TPU v7x, 512 devices: a whole 4x8x8 slice. The times are simulated.
512 devices in a mesh: row: 8 (over y), col: 64 (over z, x, core).
Axes of the slice: x: 4, y: 8, z: 8, core: 2. Of those that a mesh axis runs over, the one named last changes fastest.
Arguments:
- ppmi: bfloat16 [4096, 128256], P('row', 'col'), may hold values from -12000 to 12000
- basis: bfloat16 [256, 128256], P(None, 'col'), may hold values from -10 to 10
Outputs:
- left_basis: bfloat16 [256, 4096], P(None, 'row')
- right_basis: bfloat16 [256, 128256], P(None, 'col')
All inputs are finite; a program needn't handle non-finite values.
Results may differ from a plain program's by a relative error of at most 0.0045.
Values may be sent and summed in bfloat16 or wider, within the bound.
A program may use at most 128 MiB of HBM per device.

v0:
```python
import jax
import jax.numpy as jnp
from jax import lax
from jax.sharding import Mesh
from jax.sharding import PartitionSpec as P

COL = ("col_0", "col_1", "col_2")


def in_blocks(array, dim, peers):
    before, after = (array.shape[:dim], array.shape[dim + 1 :])
    return jnp.moveaxis(array.reshape(*before, peers, -1, *after), dim, 0)


def sum_at_owner(array, axis, dim):
    peers = lax.axis_size(axis)
    pieces = lax.all_to_all(in_blocks(array, dim, peers), axis, 0, 0, tiled=True)
    return jnp.sum(pieces, axis=0)


def summed_rows(array, axes, dim):
    far, near = axes
    pieces = in_blocks(array, dim, lax.axis_size(far))
    nearer = sum_at_owner(pieces, near, dim + 1)
    arrived = lax.all_to_all(nearer, far, split_axis=0, concat_axis=0, tiled=True)
    return arrived.sum(axis=0)


def rows_for(lines, peers):
    spare = -len(lines) % peers
    return jnp.pad(lines, [(0, spare)] + [(0, 0)] * (lines.ndim - 1))


def copy_for_each(array, axis):
    peers = lax.axis_size(axis)
    return lax.all_to_all(
        jnp.broadcast_to(array[None], (peers, *array.shape)), axis, 0, 0, tiled=True
    )


def joined_along(pieces, dim):
    shape = list(pieces.shape[1:])
    shape[dim] *= pieces.shape[0]
    return jnp.moveaxis(pieces, 0, dim).reshape(shape)


def gathered_by_axis(array, axes, dim):
    far, near = axes
    pieces = copy_for_each(copy_for_each(array, far), near)
    return joined_along(pieces.swapaxes(0, 1).reshape(-1, *array.shape), dim)


def nested_sum(array, axes):
    lines = array.reshape(-1, array.shape[-1])
    own = summed_rows(rows_for(lines, lax.axis_size(axes[0]) * lax.axis_size(axes[1])), axes, 0)
    whole = gathered_by_axis(own, axes, 0)
    return whole[: len(lines)].reshape(array.shape)


def of_everyone(array, axis):
    everything = copy_for_each(array, axis)
    return jnp.sum(everything, axis=0)


def local_gram(block):
    return jnp.dot(block, block.T, precision=lax.Precision.HIGHEST)


def solve_rows(gram, block):
    lower = jnp.linalg.cholesky(gram)
    solved = lax.linalg.triangular_solve(lower, block, left_side=True, lower=True)
    return solved.astype(jnp.bfloat16)


def local(ppmi, basis):
    rows_total = ppmi.shape[0] * lax.axis_size("row")
    cols_total = ppmi.shape[1] * lax.axis_size(COL)
    basis_now = basis
    left = None
    partial_value = lax.dot_general(
        basis_now, ppmi, (((1,), (1,)), ((), ())), preferred_element_type=jnp.float32
    )
    y_total = nested_sum(partial_value, (("col_0", "col_1"), "col_2"))
    gram_left = of_everyone(local_gram(y_total), "row") / rows_total
    left = solve_rows(gram_left, y_total)
    z_part = jnp.dot(left, ppmi, preferred_element_type=jnp.float32)
    z_total = lax.psum(z_part, "row")
    gram_right = nested_sum(local_gram(z_total), (("col_0", "col_1"), "col_2")) / cols_total
    basis_now = solve_rows(gram_right, z_total)
    return (left, basis_now)


def solution(mesh):
    split = Mesh(
        mesh.devices.reshape(mesh.shape["row"], 8, 4, 2), ("row", "col_0", "col_1", "col_2")
    )
    placed = (P("row", COL), P(None, COL))
    return jax.shard_map(
        local,
        mesh=split,
        in_specs=placed,
        out_specs=(P(None, "row"), P(None, COL)),
        check_vma=False,
    )
```

profile of v0, /device:TPU:1, one launch (start us, length us, event | category | flops | bytes accessed | tf_op | source)
XLA Modules:
  0.0 395.1 jit_solution(5545338627759966449)
XLA Ops:
  7.2 1.6 copy-done
  8.7 1.9 fusion.18
  10.7 0.1 reshape_reshape.10
  10.8 0.8 copy.40
  11.7 10.4 %all-to-all-start = ((f32[2,32,4,512]{3,2,1,0:T(4,128)}), f32[2,32,4,512]{3,2,1,0:T(4,128)S(1)}, u32[]{:S(2)}, u32[]{:S(2)}) async-start(f32[2,32,4,512]{3,2,1,0:T(4,128)} %bitcast.70), calls=%async_computation | async-start | bytes 1048576 | tf_op jit(solution)/shard_map/all_to_all | solution.py:17
  22.0 1.4 all-to-all-done
  23.4 0.2 reduce_sum.45
  23.6 18.9 %all_to_all.49 = f32[32,4,512]{2,1,0:T(4,128)S(1)} all-to-all(f32[32,4,512]{2,1,0:T(4,128)S(1)} %reduce_sum.45), channel_id=1, replica_groups=mesh['row'=8,'col_0'=8,'col_1'=4,'col_2'=2] {'col_0','col_1'}, dimensions={0} | all-to-all | bytes 524288 | tf_op jit(solution)/shard_map/all_to_all | solution.py:25
  42.6 15.0 %all_to_all.45 = f32[32,4,512]{2,1,0:T(4,128)S(1)} all-to-all(f32[32,4,512]{2,1,0:T(4,128)S(1)} %broadcast_in_dim.10), channel_id=1, replica_groups=mesh['row'=8,'col_0'=8,'col_1'=4,'col_2'=2] {'col_0','col_1'}, dimensions={0} | all-to-all | bytes 524288 | tf_op jit(solution)/shard_map/all_to_all | solution.py:36
  57.7 7.1 %all_to_all.46 = f32[2,32,4,512]{3,2,1,0:T(4,128)S(1)} all-to-all(f32[2,32,4,512]{3,2,1,0:T(4,128)S(1)} %broadcast_in_dim.11), channel_id=1, replica_groups=mesh['row'=8,'col_0'=8,'col_1'=4,'col_2'=2] {'col_2'}, dimensions={0} | all-to-all | bytes 1048576 | tf_op jit(solution)/shard_map/all_to_all | solution.py:36
  64.7 0.9 copy.27
  65.6 1.2 reshape_reshape.11
  66.8 0.6 fusion.19
  67.5 1.5 broadcast_in_dim.12
  68.9 6.8 %all-to-all-start.4 = ((f32[8,256,256]{2,1,0:T(8,128)}), f32[8,256,256]{2,1,0:T(8,128)}, u32[]{:S(2)}, u32[]{:S(2)}) async-start(f32[8,256,256]{2,1,0:T(8,128)} %broadcast_in_dim.12), calls=%async_computation.4 | async-start | bytes 4194304 | tf_op jit(solution)/shard_map/all_to_all | solution.py:36
  75.8 0.3 all-reduce.3.cloned.1.call-start
  76.2 0.1 triangular_solve.105
  76.3 0.1 triangular_solve.110
  76.4 47.8 %all-to-all-done.4 = f32[8,256,256]{2,1,0:T(8,128)} async-done(((f32[8,256,256]{2,1,0:T(8,128)}), f32[8,256,256]{2,1,0:T(8,128)}, u32[]{:S(2)}, u32[]{:S(2)}) %all-to-all-start.4) | async-done | bytes 2097184 | tf_op jit(solution)/shard_map/all_to_all | solution.py:36
  124.2 1.8 reduce_sum.47
  126.0 0.1 copy.28
  126.1 0.1 copy.29
  126.3 11.7 %cholesky.130 = f32[128,128]{1,0:T(8,128)S(1)} custom-call(f32[128,128]{1,0:T(8,128)S(1)} %cholesky.194), custom_call_target="Cholesky" | custom-call | tf_op jit(solution)/shard_map/jit(cholesky)/cholesky | solution.py:70
  138.1 9.8 %custom-call.17 = f32[1,128,128]{1,2,0:T(8,128)S(1)} custom-call(f32[1,128,128]{2,1,0:T(8,128)S(1)} %get-tuple-element.48), custom_call_target="InvertDiagBlocksLowerTriangular" | custom-call | tf_op jit(solution)/shard_map/jit(cholesky)/cholesky | solution.py:70
  147.9 0.2 constant_dynamic-update-slice_fusion.3
  148.1 0.3 convolution_subtract_fusion.3
  148.4 11.7 %cholesky.147 = f32[128,128]{1,0:T(8,128)S(1)} custom-call(f32[128,128]{1,0:T(8,128)S(1)} %convolution_subtract_fusion.3), custom_call_target="Cholesky" | custom-call | tf_op jit(solution)/shard_map/jit(cholesky)/cholesky | solution.py:70
  160.1 0.7 compare_reduce_fusion.2
  162.2 4.6 %while.2 = (s32[]{:T(128)}, f32[256,256]{1,0:T(8,128)S(1)}, s32[2,2]{1,0:T(2,128)S(1)}, f32[2,128,128]{2,1,0:T(8,128)S(1)}, s32[]{:T(128)}) while((s32[]{:T(128)}, f32[256,256]{1,0:T(8,128)S(1)}, s32[2,2]{1,0:T(2,128)S(1)}, f32[2,128,128]{2,1,0:T(8,128)S(1)}, s32[]{:T(128)}) %tuple.48), condition=%wide.while_cond, body=%wide.while_body.sunk | while | flops 2 | bytes 131189 | solution.py:71
  162.8 0.7 fusion.41
  163.5 1.3 bitcast_dynamic-update-slice_fusion.4
  164.8 0.7 fusion.41
  165.5 1.3 bitcast_dynamic-update-slice_fusion.4
  166.8 19.7 %custom-call.14 = f32[2,128,128]{1,2,0:T(8,128)S(1)} custom-call(f32[2,128,128]{2,1,0:T(8,128)S(1)} %get-tuple-element.10), custom_call_target="InvertDiagBlocksLowerTriangular" | custom-call | tf_op jit(solution)/shard_map/triangular_solve | solution.py:71
  186.5 0.4 fusion.16
  187.0 0.4 convolution_subtract_fusion.1
  187.3 0.4 convolution_convert_fusion.1
  187.8 2.0 fusion.20
  189.8 77.2 %all-reduce.3.cloned.1.call-done = f32[256,2004]{0,1:T(8,128)} async-done(((f32[256,2004]{0,1:T(8,128)}), f32[256,2004]{0,1:T(8,128)}) %all-reduce.3.cloned.1.call-update) | async-done | bytes 2052112 | tf_op jit(solution)/shard_map/psum | solution.py:87
  267.0 5.7 %fusion.21 = f32[256,256]{1,0:T(8,128)S(1)} fusion(f32[256,2004]{0,1:T(8,128)} %all-reduce.3.cloned.1.call-done), kind=kOutput, calls=%fused_computation.63 | convolution fusion | flops 1576009728 | bytes 2314240 | tf_op jit(solution)/shard_map/dot_general | solution.py:66
  272.7 0.1 reshape_reshape.12
  272.8 7.7 %all_to_all.47 = f32[2,32,4,256]{3,2,1,0:T(4,128)S(1)} all-to-all(f32[2,32,4,256]{3,2,1,0:T(4,128)S(1)} %bitcast.86), channel_id=1, replica_groups=mesh['row'=8,'col_0'=8,'col_1'=4,'col_2'=2] {'col_2'}, dimensions={0} | all-to-all | bytes 524288 | tf_op jit(solution)/shard_map/all_to_all | solution.py:17
  280.5 19.1 %all_to_all.50 = f32[32,4,256]{2,1,0:T(4,128)S(1)} all-to-all(f32[32,4,256]{2,1,0:T(4,128)S(1)} %reduce_sum.48), channel_id=1, replica_groups=mesh['row'=8,'col_0'=8,'col_1'=4,'col_2'=2] {'col_0','col_1'}, dimensions={0} | all-to-all | bytes 262144 | tf_op jit(solution)/shard_map/all_to_all | solution.py:25
  299.7 13.0 %all_to_all.51 = f32[32,4,256]{2,1,0:T(4,128)S(1)} all-to-all(f32[32,4,256]{2,1,0:T(4,128)S(1)} %broadcast_in_dim.14), channel_id=1, replica_groups=mesh['row'=8,'col_0'=8,'col_1'=4,'col_2'=2] {'col_0','col_1'}, dimensions={0} | all-to-all | bytes 262144 | tf_op jit(solution)/shard_map/all_to_all | solution.py:36
  312.7 6.6 %all_to_all.48 = f32[2,32,4,256]{3,2,1,0:T(4,128)S(1)} all-to-all(f32[2,32,4,256]{3,2,1,0:T(4,128)S(1)} %broadcast_in_dim.15), channel_id=1, replica_groups=mesh['row'=8,'col_0'=8,'col_1'=4,'col_2'=2] {'col_2'}, dimensions={0} | all-to-all | bytes 524288 | tf_op jit(solution)/shard_map/all_to_all | solution.py:36
  319.5 0.1 div.27
  319.6 0.1 copy.35
  319.8 11.7 %cholesky.164 = f32[128,128]{1,0:T(8,128)S(1)} custom-call(f32[128,128]{1,0:T(8,128)S(1)} %cholesky.197), custom_call_target="Cholesky" | custom-call | tf_op jit(solution)/shard_map/jit(cholesky)/cholesky | solution.py:70
  331.5 0.7 compare_reduce_fusion.1
  332.2 9.8 %custom-call.18 = f32[1,128,128]{1,2,0:T(8,128)S(1)} custom-call(f32[1,128,128]{2,1,0:T(8,128)S(1)} %get-tuple-element.44), custom_call_target="InvertDiagBlocksLowerTriangular" | custom-call | tf_op jit(solution)/shard_map/jit(cholesky)/cholesky | solution.py:70
  342.1 0.2 constant_dynamic-update-slice_fusion.1
  342.3 0.3 convolution_subtract_fusion.2
  342.5 11.7 %cholesky.181 = f32[128,128]{1,0:T(8,128)S(1)} custom-call(f32[128,128]{1,0:T(8,128)S(1)} %convolution_subtract_fusion.2), custom_call_target="Cholesky" | custom-call | tf_op jit(solution)/shard_map/jit(cholesky)/cholesky | solution.py:70
  354.3 0.6 compare_reduce_fusion
  356.2 4.1 %while.3 = (s32[]{:T(128)}, f32[256,256]{1,0:T(8,128)S(1)}, s32[2,2]{1,0:T(2,128)S(1)}, f32[2,128,128]{2,1,0:T(8,128)S(1)}, s32[]{:T(128)}) while((s32[]{:T(128)}, f32[256,256]{1,0:T(8,128)S(1)}, s32[2,2]{1,0:T(2,128)S(1)}, f32[2,128,128]{2,1,0:T(8,128)S(1)}, s32[]{:T(128)}) %tuple.56), condition=%wide.while_cond.1, body=%wide.while_body.1.sunk | while | flops 2 | bytes 131189 | solution.py:71
  356.3 0.7 fusion.42
  356.9 1.3 bitcast_dynamic-update-slice_fusion.5
  358.3 0.7 fusion.42
  359.0 1.3 bitcast_dynamic-update-slice_fusion.5
  360.3 19.9 %custom-call.15 = f32[2,128,128]{1,2,0:T(8,128)S(1)} custom-call(f32[2,128,128]{2,1,0:T(8,128)S(1)} %get-tuple-element.18), custom_call_target="InvertDiagBlocksLowerTriangular" | custom-call | tf_op jit(solution)/shard_map/triangular_solve | solution.py:71
  380.2 3.1 fusion.17
  383.4 1.8 convolution_subtract_fusion
  385.2 1.7 convolution_convert_fusion
  386.9 1.1 pad_maximum_fusion
  (41 shorter events, 1.0 us)
Async XLA Ops:
  7.2 1.6 copy-start
  11.7 11.7 %all-to-all-start = ((f32[2,32,4,512]{3,2,1,0:T(4,128)}), f32[2,32,4,512]{3,2,1,0:T(4,128)S(1)}, u32[]{:S(2)}, u32[]{:S(2)}) async-start(f32[2,32,4,512]{3,2,1,0:T(4,128)} %bitcast.70), calls=%async_computation | async-start | bytes 1048576 | tf_op jit(solution)/shard_map/all_to_all | solution.py:17
  68.9 55.3 %all-to-all-start.4 = ((f32[8,256,256]{2,1,0:T(8,128)}), f32[8,256,256]{2,1,0:T(8,128)}, u32[]{:S(2)}, u32[]{:S(2)}) async-start(f32[8,256,256]{2,1,0:T(8,128)} %broadcast_in_dim.12), calls=%async_computation.4 | async-start | bytes 4194304 | tf_op jit(solution)/shard_map/all_to_all | solution.py:36
  75.8 191.3 %all-reduce.3.cloned.1.call-start = ((), (), s32[]{:S(2)}) async-start(), calls=%async_computation.9 | async-start | bytes 4112384 | tf_op jit(solution)/shard_map/psum | solution.py:87
  187.8 2.0 copy-start.2
  380.2 3.1 copy-start.1
Sparse Core Ops, SparseCore 0:
  190.0 77.0 all-reduce.2
where the time goes:
time: 399 us; the launch traced here: 395 us
  waiting for transfers between devices  126 us (32%)
  other arithmetic  112 us (28%)
  blocking collectives  87.3 us (22%)
  matrix products  19.1 us (5%)
  starting transfers between devices  17.5 us (4%)
  between operations  17.2 us (4%)
  local copies, waits for them, and re-layouts  15.3 us (4%)
    psum x1, waiting for transfers between devices, local(): z_total = lax.psum(z_part, 'row')  77.2 us
    another operation x13, other arithmetic, solve_rows(): lower = jnp.linalg.cholesky(gram)  68.7 us
    all_to_all x1, waiting for transfers between devices, copy_for_each(): lax.all_to_all(jnp.broadcast_to(array[None], (peers, *array.shape)), axis...  47.8 us
    all_to_all x4, blocking collectives, copy_for_each(): lax.all_to_all(jnp.broadcast_to(array[None], (peers, *array.shape)), axis...  41.7 us
    another operation x7, other arithmetic, solve_rows(): lax.linalg.triangular_solve(lower, block, left_side=True, lower=True)  40.7 us
    all_to_all x2, blocking collectives, summed_rows(): lax.all_to_all(nearer, far, split_axis=0, concat_axis=0, tiled=True)  37.9 us
    all_to_all x1, starting transfers between devices, sum_at_owner(): lax.all_to_all(in_blocks(array, dim, peers), axis, 0, 0, tiled=True)  10.4 us
    another operation x12, local copies, waits for them, and re-layouts  8.04 us
  transfers between devices with their start and end apart: 3, of which 3 were waited for; matrix products, arithmetic and copies ran while one was open for 0% of the time, Pallas kernels for 0%

commit v1 on v0

--- a/solution.py
+++ b/solution.py
@@ -84,7 +84,9 @@
     gram_left = of_everyone(local_gram(y_total), "row") / rows_total
     left = solve_rows(gram_left, y_total)
     z_part = jnp.dot(left, ppmi, preferred_element_type=jnp.float32)
-    z_total = lax.psum(z_part, "row")
+    z_total = z_part
+    for hop in (1, 2, 4):
+        z_total = z_total + lax.ppermute(z_total, "row", [(dev, dev ^ hop) for dev in range(8)])
     gram_right = nested_sum(local_gram(z_total), (("col_0", "col_1"), "col_2")) / cols_total
     basis_now = solve_rows(gram_right, z_total)
     return (left, basis_now)

time: 399 us -> 534 us (1.34)
  waiting for transfers between devices: 126 us -> 267 us
  starting transfers between devices: 17.5 us -> 33.8 us
  between operations: 17.2 us -> 3.82 us
  blocking collectives: 87.3 us -> 79.8 us
    ppermute x0 -> x3, waiting for transfers between devices: none -> 217 us  [local(): lax.ppermute(z_total, 'row', [(dev, dev ^ hop) for dev in range(8)])]
    psum x1 -> x0, waiting for transfers between devices: 77.2 us -> none  [local(): z_total = lax.psum(z_part, 'row')]
    ppermute x0 -> x3, starting transfers between devices: none -> 16.3 us  [local(): lax.ppermute(z_total, 'row', [(dev, dev ^ hop) for dev in range(8)])]
    all_to_all x2, blocking collectives: 37.9 us -> 31.6 us  [summed_rows(): lax.all_to_all(nearer, far, split_axis=0, concat_axis=0, tiled=True)]
  transfers between devices with their start and end apart: 3 -> 5, of which waited for: 3 -> 5; matrix products, arithmetic and copies ran while one was open for 0% -> 0% of each run, Pallas kernels for 0% -> 0%
where the time goes in v1:
time: 534 us; the launch traced here: 530 us
  waiting for transfers between devices  267 us (50%)
  other arithmetic  113 us (21%)
  blocking collectives  79.8 us (15%)
  starting transfers between devices  33.8 us (6%)
  local copies, waits for them, and re-layouts  16.6 us (3%)
  matrix products  15.6 us (3%)
    ppermute x3, waiting for transfers between devices, local(): lax.ppermute(z_total, 'row', [(dev, dev ^ hop) for dev in range(8)])  217 us
    another operation x13, other arithmetic, solve_rows(): lower = jnp.linalg.cholesky(gram)  68.7 us
    all_to_all x1, waiting for transfers between devices, copy_for_each(): lax.all_to_all(jnp.broadcast_to(array[None], (peers, *array.shape)), axis...  48.1 us
    all_to_all x4, blocking collectives, copy_for_each(): lax.all_to_all(jnp.broadcast_to(array[None], (peers, *array.shape)), axis...  41.7 us
    another operation x7, other arithmetic, solve_rows(): lax.linalg.triangular_solve(lower, block, left_side=True, lower=True)  41.2 us
    all_to_all x2, blocking collectives, summed_rows(): lax.all_to_all(nearer, far, split_axis=0, concat_axis=0, tiled=True)  31.6 us
    ppermute x3, starting transfers between devices, local(): lax.ppermute(z_total, 'row', [(dev, dev ^ hop) for dev in range(8)])  16.3 us
  transfers between devices with their start and end apart: 5, of which 5 were waited for; matrix products, arithmetic and copies ran while one was open for 0% of the time, Pallas kernels for 0%

profile of v1, /device:TPU:1, one launch (start us, length us, event | category | flops | bytes accessed | tf_op | source)
XLA Modules:
  0.0 529.7 jit_solution(13747374498108699659)
XLA Ops:
  0.6 1.6 copy-done
  2.2 1.9 fusion.19
  4.3 0.8 copy.40
  5.1 10.4 %all-to-all-start = ((f32[2,32,4,512]{3,2,1,0:T(4,128)}), f32[2,32,4,512]{3,2,1,0:T(4,128)S(1)}, u32[]{:S(2)}, u32[]{:S(2)}) async-start(f32[2,32,4,512]{3,2,1,0:T(4,128)} %bitcast.69), calls=%async_computation | async-start | bytes 1048576 | tf_op jit(solution)/shard_map/all_to_all | solution.py:17
  15.5 1.4 all-to-all-done
  16.9 0.2 reduce_sum.45
  17.1 18.9 %all_to_all.49 = f32[32,4,512]{2,1,0:T(4,128)S(1)} all-to-all(f32[32,4,512]{2,1,0:T(4,128)S(1)} %reduce_sum.45), channel_id=1, replica_groups=mesh['row'=8,'col_0'=8,'col_1'=4,'col_2'=2] {'col_0','col_1'}, dimensions={0} | all-to-all | bytes 524288 | tf_op jit(solution)/shard_map/all_to_all | solution.py:25
  36.1 15.0 %all_to_all.45 = f32[32,4,512]{2,1,0:T(4,128)S(1)} all-to-all(f32[32,4,512]{2,1,0:T(4,128)S(1)} %broadcast_in_dim.10), channel_id=1, replica_groups=mesh['row'=8,'col_0'=8,'col_1'=4,'col_2'=2] {'col_0','col_1'}, dimensions={0} | all-to-all | bytes 524288 | tf_op jit(solution)/shard_map/all_to_all | solution.py:36
  51.1 7.1 %all_to_all.46 = f32[2,32,4,512]{3,2,1,0:T(4,128)S(1)} all-to-all(f32[2,32,4,512]{3,2,1,0:T(4,128)S(1)} %broadcast_in_dim.11), channel_id=1, replica_groups=mesh['row'=8,'col_0'=8,'col_1'=4,'col_2'=2] {'col_2'}, dimensions={0} | all-to-all | bytes 1048576 | tf_op jit(solution)/shard_map/all_to_all | solution.py:36
  58.2 0.9 copy.27
  59.1 1.2 reshape_reshape.11
  60.3 0.6 fusion.20
  60.9 1.5 broadcast_in_dim.12
  62.4 7.2 %all-to-all-start.4 = ((f32[8,256,256]{2,1,0:T(8,128)}), f32[8,256,256]{2,1,0:T(8,128)}, u32[]{:S(2)}, u32[]{:S(2)}) async-start(f32[8,256,256]{2,1,0:T(8,128)} %broadcast_in_dim.12), calls=%async_computation.4 | async-start | bytes 4194304 | tf_op jit(solution)/shard_map/all_to_all | solution.py:36
  69.9 48.1 %all-to-all-done.4 = f32[8,256,256]{2,1,0:T(8,128)} async-done(((f32[8,256,256]{2,1,0:T(8,128)}), f32[8,256,256]{2,1,0:T(8,128)}, u32[]{:S(2)}, u32[]{:S(2)}) %all-to-all-start.4) | async-done | bytes 2097184 | tf_op jit(solution)/shard_map/all_to_all | solution.py:36
  117.9 1.8 reduce_sum.47
  120.1 11.7 %cholesky.130 = f32[128,128]{1,0:T(8,128)S(1)} custom-call(f32[128,128]{1,0:T(8,128)S(1)} %cholesky.194), custom_call_target="Cholesky" | custom-call | tf_op jit(solution)/shard_map/jit(cholesky)/cholesky | solution.py:70
  131.8 9.8 %custom-call.17 = f32[1,128,128]{1,2,0:T(8,128)S(1)} custom-call(f32[1,128,128]{2,1,0:T(8,128)S(1)} %get-tuple-element.48), custom_call_target="InvertDiagBlocksLowerTriangular" | custom-call | tf_op jit(solution)/shard_map/jit(cholesky)/cholesky | solution.py:70
  141.7 0.2 constant_dynamic-update-slice_fusion.3
  141.9 0.3 convolution_subtract_fusion.2
  142.1 11.7 %cholesky.147 = f32[128,128]{1,0:T(8,128)S(1)} custom-call(f32[128,128]{1,0:T(8,128)S(1)} %convolution_subtract_fusion.2), custom_call_target="Cholesky" | custom-call | tf_op jit(solution)/shard_map/jit(cholesky)/cholesky | solution.py:70
  153.9 0.7 compare_reduce_fusion.2
  156.0 4.1 while.2
  156.0 0.7 fusion.41
  156.7 1.3 bitcast_dynamic-update-slice_fusion.4
  158.1 0.7 fusion.41
  158.7 1.3 bitcast_dynamic-update-slice_fusion.4
  160.1 20.2 %custom-call.14 = f32[2,128,128]{1,2,0:T(8,128)S(1)} custom-call(f32[2,128,128]{2,1,0:T(8,128)S(1)} %get-tuple-element.10), custom_call_target="InvertDiagBlocksLowerTriangular" | custom-call | tf_op jit(solution)/shard_map/triangular_solve | solution.py:71
  180.3 0.4 fusion.17
  180.7 0.4 convolution_subtract_fusion
  181.1 0.4 convolution_convert_fusion.1
  181.5 0.7 fusion.21
  182.3 4.5 collective-permute-start
  186.8 42.5 %collective-permute-done = f32[256,2004]{0,1:T(8,128)S(1)} collective-permute-done((f32[256,2004]{0,1:T(8,128)S(1)}, f32[256,2004]{0,1:T(8,128)S(1)}, u32[]{:S(2)}, u32[]{:S(2)}) %collective-permute-start) | collective-permute-done | bytes 2052128 | tf_op jit(solution)/shard_map/ppermute | solution.py:89
  229.3 0.4 add.29
  229.7 4.3 collective-permute-start.1
  234.0 87.4 %collective-permute-done.1 = f32[256,2004]{0,1:T(8,128)S(1)} collective-permute-done((f32[256,2004]{0,1:T(8,128)S(1)}, f32[256,2004]{0,1:T(8,128)S(1)}, u32[]{:S(2)}, u32[]{:S(2)}) %collective-permute-start.1) | collective-permute-done | bytes 2052128 | tf_op jit(solution)/shard_map/ppermute | solution.py:89
  321.4 0.3 add.30
  321.7 7.4 %collective-permute-start.2 = (f32[256,2004]{0,1:T(8,128)S(1)}, f32[256,2004]{0,1:T(8,128)S(1)}, u32[]{:S(2)}, u32[]{:S(2)}) collective-permute-start(f32[256,2004]{0,1:T(8,128)S(1)} %add.30), channel_id=1, source_target_pairs={{0,256},{64,320},{128,384},{192,448},{256,0},{320,64},{384,128},{4... | collective-permute-start | bytes 6156296 | tf_op jit(solution)/shard_map/ppermute | solution.py:89
  329.1 87.5 %collective-permute-done.2 = f32[256,2004]{0,1:T(8,128)S(1)} collective-permute-done((f32[256,2004]{0,1:T(8,128)S(1)}, f32[256,2004]{0,1:T(8,128)S(1)}, u32[]{:S(2)}, u32[]{:S(2)}) %collective-permute-start.2) | collective-permute-done | bytes 2052128 | tf_op jit(solution)/shard_map/ppermute | solution.py:89
  416.6 0.4 add.31
  417.0 1.3 copy-done.1
  418.3 3.5 fusion.22
  421.9 6.5 %all_to_all.47 = f32[2,32,4,256]{3,2,1,0:T(4,128)S(1)} all-to-all(f32[2,32,4,256]{3,2,1,0:T(4,128)S(1)} %bitcast.85), channel_id=1, replica_groups=mesh['row'=8,'col_0'=8,'col_1'=4,'col_2'=2] {'col_2'}, dimensions={0} | all-to-all | bytes 524288 | tf_op jit(solution)/shard_map/all_to_all | solution.py:17
  428.4 12.7 %all_to_all.50 = f32[32,4,256]{2,1,0:T(4,128)S(1)} all-to-all(f32[32,4,256]{2,1,0:T(4,128)S(1)} %reduce_sum.48), channel_id=1, replica_groups=mesh['row'=8,'col_0'=8,'col_1'=4,'col_2'=2] {'col_0','col_1'}, dimensions={0} | all-to-all | bytes 262144 | tf_op jit(solution)/shard_map/all_to_all | solution.py:25
  441.2 13.0 %all_to_all.51 = f32[32,4,256]{2,1,0:T(4,128)S(1)} all-to-all(f32[32,4,256]{2,1,0:T(4,128)S(1)} %broadcast_in_dim.14), channel_id=1, replica_groups=mesh['row'=8,'col_0'=8,'col_1'=4,'col_2'=2] {'col_0','col_1'}, dimensions={0} | all-to-all | bytes 262144 | tf_op jit(solution)/shard_map/all_to_all | solution.py:36
  454.2 6.6 %all_to_all.48 = f32[2,32,4,256]{3,2,1,0:T(4,128)S(1)} all-to-all(f32[2,32,4,256]{3,2,1,0:T(4,128)S(1)} %broadcast_in_dim.15), channel_id=1, replica_groups=mesh['row'=8,'col_0'=8,'col_1'=4,'col_2'=2] {'col_2'}, dimensions={0} | all-to-all | bytes 524288 | tf_op jit(solution)/shard_map/all_to_all | solution.py:36
  461.3 11.7 %cholesky.164 = f32[128,128]{1,0:T(8,128)S(1)} custom-call(f32[128,128]{1,0:T(8,128)S(1)} %cholesky.197), custom_call_target="Cholesky" | custom-call | tf_op jit(solution)/shard_map/jit(cholesky)/cholesky | solution.py:70
  473.0 0.7 compare_reduce_fusion.1
  473.7 9.8 %custom-call.18 = f32[1,128,128]{1,2,0:T(8,128)S(1)} custom-call(f32[1,128,128]{2,1,0:T(8,128)S(1)} %get-tuple-element.44), custom_call_target="InvertDiagBlocksLowerTriangular" | custom-call | tf_op jit(solution)/shard_map/jit(cholesky)/cholesky | solution.py:70
  483.6 0.2 constant_dynamic-update-slice_fusion.1
  483.8 0.3 convolution_subtract_fusion.1
  484.0 11.7 %cholesky.181 = f32[128,128]{1,0:T(8,128)S(1)} custom-call(f32[128,128]{1,0:T(8,128)S(1)} %convolution_subtract_fusion.1), custom_call_target="Cholesky" | custom-call | tf_op jit(solution)/shard_map/jit(cholesky)/cholesky | solution.py:70
  495.8 0.6 compare_reduce_fusion
  497.7 4.1 while.3
  497.8 0.7 fusion.42
  498.4 1.3 bitcast_dynamic-update-slice_fusion.5
  499.8 0.7 fusion.42
  500.5 1.3 bitcast_dynamic-update-slice_fusion.5
  501.8 19.9 %custom-call.15 = f32[2,128,128]{1,2,0:T(8,128)S(1)} custom-call(f32[2,128,128]{2,1,0:T(8,128)S(1)} %get-tuple-element.18), custom_call_target="InvertDiagBlocksLowerTriangular" | custom-call | tf_op jit(solution)/shard_map/triangular_solve | solution.py:71
  521.7 3.1 fusion.18
  524.9 1.8 fusion.4
  526.6 1.8 convolution_convert_fusion
  528.4 1.1 pad_maximum_fusion
  (49 shorter events, 1.9 us)
Async XLA Ops:
  0.6 1.6 copy-start
  5.1 11.7 %all-to-all-start = ((f32[2,32,4,512]{3,2,1,0:T(4,128)}), f32[2,32,4,512]{3,2,1,0:T(4,128)S(1)}, u32[]{:S(2)}, u32[]{:S(2)}) async-start(f32[2,32,4,512]{3,2,1,0:T(4,128)} %bitcast.69), calls=%async_computation | async-start | bytes 1048576 | tf_op jit(solution)/shard_map/all_to_all | solution.py:17
  62.4 55.6 %all-to-all-start.4 = ((f32[8,256,256]{2,1,0:T(8,128)}), f32[8,256,256]{2,1,0:T(8,128)}, u32[]{:S(2)}, u32[]{:S(2)}) async-start(f32[8,256,256]{2,1,0:T(8,128)} %broadcast_in_dim.12), calls=%async_computation.4 | async-start | bytes 4194304 | tf_op jit(solution)/shard_map/all_to_all | solution.py:36
  181.5 0.7 copy-start.3
  182.3 47.0 %collective-permute-start = (f32[256,2004]{0,1:T(8,128)S(1)}, f32[256,2004]{0,1:T(8,128)S(1)}, u32[]{:S(2)}, u32[]{:S(2)}) collective-permute-start(f32[256,2004]{0,1:T(8,128)S(1)} %fusion.21), channel_id=1, source_target_pairs={{0,64},{64,0},{128,192},{192,128},{256,320},{320,256},{384,448},{4... | collective-permute-start | bytes 6156296 | tf_op jit(solution)/shard_map/ppermute | solution.py:89
  229.7 91.7 %collective-permute-start.1 = (f32[256,2004]{0,1:T(8,128)S(1)}, f32[256,2004]{0,1:T(8,128)S(1)}, u32[]{:S(2)}, u32[]{:S(2)}) collective-permute-start(f32[256,2004]{0,1:T(8,128)S(1)} %add.29), channel_id=1, source_target_pairs={{0,128},{64,192},{128,0},{192,64},{256,384},{320,448},{384,256},{4... | collective-permute-start | bytes 6156296 | tf_op jit(solution)/shard_map/ppermute | solution.py:89
  321.7 94.9 %collective-permute-start.2 = (f32[256,2004]{0,1:T(8,128)S(1)}, f32[256,2004]{0,1:T(8,128)S(1)}, u32[]{:S(2)}, u32[]{:S(2)}) collective-permute-start(f32[256,2004]{0,1:T(8,128)S(1)} %add.30), channel_id=1, source_target_pairs={{0,256},{64,320},{128,384},{192,448},{256,0},{320,64},{384,128},{4... | collective-permute-start | bytes 6156296 | tf_op jit(solution)/shard_map/ppermute | solution.py:89
  417.0 1.3 copy-start.1
  521.7 4.9 copy-start.2
